TPU v7x, 32 devices: a whole 2x2x4 slice. The times are simulated.
32 devices in a mesh: layer: 2 (over x), expert: 4 (over y, core), col: 4 (over z).
Axes of the slice: x: 2, y: 2, z: 4, core: 2. Of those that a mesh axis runs over, the one named last changes fastest.
Arguments:
- target_weights: bfloat16 [8, 7168, 2048], P(('layer', 'expert'), None, 'col'), parts along dimension 0, may hold values from -36 to 36
- factors: float32 [8, 7168, 128], P(('layer', 'expert'), 'col'), parts along dimension 0, may hold values from -0.5 to 0.5
- bases: float32 [64, 128, 2048], P('layer', None, 'col'), parts along dimension 0, may hold values from -6 to 6
- coefficients: float32 [8, 32], P(('layer', 'expert')), parts along dimension 0, may hold values from -1 to 1
Outputs:
- new_factors: float32 [8, 7168, 128], P(('layer', 'expert'), 'col'), parts along dimension 0
- new_bases: float32 [64, 128, 2048], P('layer', None, 'col'), parts along dimension 0
- new_coefficients: float32 [8, 32], P(('layer', 'expert')), parts along dimension 0
- losses: float32 [4], P('layer'), parts along dimension 0
There are 2 independent parts, one for each index of `layer`. A program takes and returns all parts, laid end to end along the dimension named above; each array names one. Nothing has to cross between parts.
All inputs are finite; a program needn't handle non-finite values.
Results may differ from a plain program's by a relative error of at most 0.0003.
Values sent between devices are 32-bit elements; how exact they have to be, the bound alone decides.
A program may use at most 128 MiB of HBM per device.

v0:
```python
import jax
import jax.numpy as jnp
from jax import lax
from jax.sharding import PartitionSpec as P

D = 7168
H = 2048
ITERS = 2
LEARN_RATE = 0.01
BETA_ONE = 0.9
BETA_TWO = 0.999
EPSILON = 0.0001
HIGHEST = lax.Precision.HIGHEST


def adam_update(parameter, gradient, moment_one, moment_two, iteration):
    moment_one = BETA_ONE * moment_one + (1.0 - BETA_ONE) * gradient
    moment_two = BETA_TWO * moment_two + (1.0 - BETA_TWO) * gradient * gradient
    first_hat = moment_one / (1.0 - BETA_ONE ** (iteration + 1))
    second_hat = moment_two / (1.0 - BETA_TWO ** (iteration + 1))
    parameter = parameter - LEARN_RATE * first_hat / (jnp.sqrt(second_hat) + EPSILON)
    return (parameter, moment_one, moment_two)


def shards(target_weights, factors, bases, coefficients):
    expert_count = lax.axis_size("expert")
    local_experts = target_weights.shape[0]
    basis_share = bases.shape[0] // expert_count
    basis_begin = lax.axis_index("expert") * basis_share
    loss_scale = 1.0 / (2.0 * local_experts * expert_count * D * H)
    own_bases = lax.dynamic_slice_in_dim(bases, basis_begin, basis_share, 0)
    basis_one = jnp.zeros_like(own_bases)
    basis_two = jnp.zeros_like(own_bases)
    coef_one = jnp.zeros_like(coefficients)
    coef_two = jnp.zeros_like(coefficients)
    current_bases = bases
    current_factors = factors
    factor_one = jnp.zeros_like(factors)
    factor_two = jnp.zeros_like(factors)
    loss_values = []
    for iteration in range(ITERS):
        gathered = lax.all_gather(current_factors, "col", axis=1, tiled=True)
        mixed = jnp.tanh(jnp.einsum("ek,krh->erh", coefficients, current_bases, precision=HIGHEST))
        residual = jnp.einsum(
            "edr,erh->edh", gathered, mixed, precision=HIGHEST
        ) - target_weights.astype(jnp.float32)
        loss_part = jnp.sum(residual * residual)
        gradient = residual / H
        d_mixed = jnp.einsum("edr,edh->erh", gathered, gradient, precision=HIGHEST)
        d_pre = d_mixed * (1.0 - mixed * mixed)
        coef_slice = coefficients
        d_basis = lax.psum_scatter(
            jnp.einsum("ek,erh->krh", coef_slice, d_pre, precision=HIGHEST),
            "expert",
            scatter_dimension=0,
            tiled=True,
        )
        d_coef = lax.psum(jnp.einsum("krh,erh->ek", current_bases, d_pre, precision=HIGHEST), "col")
        d_share = lax.psum_scatter(
            jnp.einsum("edh,erh->der", gradient, mixed, precision=HIGHEST),
            "col",
            scatter_dimension=0,
            tiled=True,
        )
        d_share = jnp.transpose(d_share, (1, 0, 2))
        current_factors, factor_one, factor_two = adam_update(
            current_factors, d_share, factor_one, factor_two, iteration
        )
        own_bases, basis_one, basis_two = adam_update(
            own_bases, d_basis, basis_one, basis_two, iteration
        )
        coefficients, coef_one, coef_two = adam_update(
            coefficients, d_coef, coef_one, coef_two, iteration
        )
        current_bases = lax.all_gather(own_bases, "expert", axis=0, tiled=True)
        loss_values.append(lax.psum(loss_part, ("expert", "col")))
    loss_totals = jnp.stack(loss_values)
    return (current_factors, current_bases, coefficients, loss_totals * loss_scale)


def solution(mesh):
    return jax.shard_map(
        shards,
        mesh=mesh,
        in_specs=(
            P(("layer", "expert"), None, "col"),
            P(("layer", "expert"), "col", None),
            P("layer", None, "col"),
            P(("layer", "expert"), None),
        ),
        out_specs=(
            P(("layer", "expert"), "col", None),
            P("layer", None, "col"),
            P(("layer", "expert"), None),
            P("layer"),
        ),
        check_vma=False,
    )
```

profile of v0, /device:TPU:0, one launch (start us, length us, event | category | flops | bytes accessed | tf_op | source)
XLA Modules:
  0.0 658.7 jit_solution(1172919864465616903)
XLA Ops:
  7.9 12.3 %fusion.20 = f32[1,128,512]{2,0,1:T(1,128)S(1)} fusion(f32[32,128,512]{2,1,0:T(8,128)} %param.6, f32[1,32]{1,0:T(1,128)} %param.7), kind=kOutput, calls=%fused_computation.20 | convolution fusion | flops 25165824 | bytes 8650880 | tf_op jit(solution)/shard_map/ek,krh->erh/dot_general | solution.py:43
  20.4 10.1 %copy.15 = bf16[1,7168,512]{1,2,0:T(8,128)(2,1)} copy(bf16[1,7168,512]{2,1,0:T(8,128)(2,1)} %param.4) | data formatting | bytes 14680064 | tf_op args[0]
  30.4 54.0 %all-gather.5.cloned.1.call-done = f32[1,7168,128]{2,1,0:T(8,128)} async-done(((f32[1,1792,128]{2,1,0:T(8,128)}), f32[1,7168,128]{2,1,0:T(8,128)}) %all-gather.5.cloned.1.call-update) | async-done | bytes 3670032 | tf_op jit(solution)/shard_map/all_gather | solution.py:42
  84.4 19.3 %multiply_reduce_fusion.1 = (f32[]{:T(128)}, f32[1,7168,512]{1,2,0:T(8,128)S(1)}) fusion(bf16[1,7168,512]{1,2,0:T(8,128)(2,1)} %copy.15, f32[1,7168,128]{2,1,0:T(8,128)} %all-gather.5.cloned.1.call-done, f32[1,128,512]{1,2,0:T(8,128)S(1)} %copy.23), kind=kOutput, calls=%fused_computation.11 | convolution fusion | flops 5651824640 | bytes 25952260 | tf_op jit(solution)/shard_map/edr,erh->edh/dot_general | solution.py:44
  108.9 11.7 %fusion.41 = f32[128,512]{0,1:T(8,128)S(1)} fusion(f32[1,7168,128]{2,1,0:T(8,128)S(1)} %copy-done.4, f32[1,7168,512]{1,2,0:T(8,128)S(1)} %get-tuple-element.17, f32[1,128,512]{1,2,0:T(8,128)S(1)} %copy.23), kind=kOutput, calls=%fused_computation.44 | convolution fusion | flops 5641011200 | bytes 18874368 | tf_op jit(solution)/shard_map/edr,edh->erh/dot_general | solution.py:49
  125.4 13.9 %fusion.12 = f32[7168,1,128]{0,2,1:T(8,128)} fusion(f32[1,7168,512]{1,2,0:T(8,128)} %copy-done.1, f32[1,128,512]{1,2,0:T(8,128)S(1)} %copy.23), kind=kOutput, calls=%fused_computation.16 | convolution fusion | flops 5640814592 | bytes 18612224 | tf_op jit(solution)/shard_map/edh,erh->der/dot_general | solution.py:60
  139.3 56.1 %reduce-scatter.7.cloned.1.call-done = f32[8,128,512]{2,1,0:T(8,128)} async-done(((f32[32,128,512]{2,1,0:T(8,128)}), f32[8,128,512]{2,1,0:T(8,128)}) %reduce-scatter.7.cloned.1.call-update) | async-done | bytes 2097168 | tf_op jit(solution)/shard_map/reduce_scatter | solution.py:52
  200.4 65.9 %reduce-scatter.5.cloned.1.call-done = f32[1792,1,128]{0,2,1:T(8,128)} async-done(((f32[7168,1,128]{0,2,1:T(8,128)}), f32[1792,1,128]{0,2,1:T(8,128)}) %reduce-scatter.5.cloned.1.call-update) | async-done | bytes 917520 | tf_op jit(solution)/shard_map/reduce_scatter | solution.py:59
  268.9 10.5 %copy.25 = f32[32,128,512]{1,0,2:T(8,128)} copy(f32[32,128,512]{2,1,0:T(8,128)} %param.6) | data formatting | bytes 16777216 | tf_op args[2]
  279.5 9.3 %convolution_bitcast_fusion.1 = f32[1,32]{1,0:T(1,128)S(1)} fusion(f32[128,512,1]{0,2,1:T(1,128)S(1)} %bitcast.131, f32[32,128,512]{1,0,2:T(8,128)} %copy.25), kind=kOutput, calls=%fused_computation.47 | convolution fusion | flops 25165824 | bytes 8650880 | tf_op jit(solution)/shard_map/krh,erh->ek/dot_general | solution.py:58
  288.8 11.5 %psum.28 = f32[1,32]{1,0:T(1,128)S(1)} all-reduce(f32[1,32]{1,0:T(1,128)S(1)} %convolution_bitcast_fusion.1), channel_id=1, replica_groups=mesh['layer'=2,'expert'=4,'col'=4] {'col'}, use_global_device_ids=true, to_apply=%region_1.0 | all-reduce | flops 32 | bytes 256 | tf_op jit(solution)/shard_map/psum | solution.py:58
  300.3 26.0 %all-gather.7.cloned.1.call-done = f32[32,128,512]{2,1,0:T(8,128)} async-done(((f32[8,128,512]{2,1,0:T(8,128)}), f32[32,128,512]{2,1,0:T(8,128)}) %all-gather.7.cloned.1.call-update) | async-done | bytes 8388624 | tf_op jit(solution)/shard_map/all_gather | solution.py:75
  326.3 12.3 %fusion.18 = f32[1,128,512]{2,0,1:T(1,128)S(1)} fusion(f32[32,128,512]{2,1,0:T(8,128)} %all-gather.7.cloned.1.call-done, f32[1,32]{1,0:T(1,128)S(1)} %divide_subtract_fusion.2), kind=kOutput, calls=%fused_computation.18 | convolution fusion | flops 25165824 | bytes 8650880 | tf_op jit(solution)/shard_map/ek,krh->erh/dot_general | solution.py:43
  338.7 61.7 %all-gather.9.cloned.1.call-done = f32[1,7168,128]{1,2,0:T(8,128)} async-done(((f32[1,1792,128]{1,2,0:T(8,128)}), f32[1,7168,128]{1,2,0:T(8,128)}) %all-gather.9.cloned.1.call-update) | async-done | bytes 3670032 | tf_op jit(solution)/shard_map/all_gather | solution.py:42
  400.4 18.9 %multiply_reduce_fusion = (f32[]{:T(128)}, f32[1,7168,512]{1,2,0:T(8,128)S(1)}) fusion(bf16[1,7168,512]{1,2,0:T(8,128)(2,1)} %copy.15, f32[1,128,512]{1,2,0:T(8,128)S(1)} %copy.27, f32[1,7168,128]{1,2,0:T(8,128)} %all-gather.9.cloned.1.call-done), kind=kOutput, calls=%fused_computation.10 | convolution fusion | flops 5651824640 | bytes 25952260 | tf_op jit(solution)/shard_map/edr,erh->edh/dot_general | solution.py:44
  424.5 11.7 %fusion.46 = f32[128,512]{0,1:T(8,128)S(1)} fusion(f32[1,7168,512]{1,2,0:T(8,128)S(1)} %get-tuple-element.15, f32[1,7168,128]{1,2,0:T(8,128)S(1)} %copy-done.2, f32[1,128,512]{1,2,0:T(8,128)S(1)} %copy.27), kind=kOutput, calls=%fused_computation.45 | convolution fusion | flops 5641011200 | bytes 18874368 | tf_op jit(solution)/shard_map/edr,edh->erh/dot_general | solution.py:49
  440.9 14.0 %fusion.15 = f32[7168,1,128]{0,2,1:T(8,128)} fusion(f32[1,7168,512]{1,2,0:T(8,128)} %copy-done, f32[1,128,512]{1,2,0:T(8,128)S(1)} %copy.27), kind=kOutput, calls=%fused_computation.17 | convolution fusion | flops 5640814592 | bytes 18612224 | tf_op jit(solution)/shard_map/edh,erh->der/dot_general | solution.py:60
  455.0 56.0 %reduce-scatter.11.cloned.1.call-done = f32[8,128,512]{2,1,0:T(8,128)} async-done(((f32[32,128,512]{2,1,0:T(8,128)}), f32[8,128,512]{2,1,0:T(8,128)}) %reduce-scatter.11.cloned.1.call-update) | async-done | bytes 2097168 | tf_op jit(solution)/shard_map/reduce_scatter | solution.py:52
  516.1 35.0 %all-reduce = (f32[1]{0:T(128)}, f32[1]{0:T(128)}) all-reduce(f32[1]{0:T(128)} %bitcast.30, f32[1]{0:T(128)} %bitcast.29), channel_id=1, replica_groups=mesh['layer'=2,'expert'=4,'col'=4] {'expert','col'}, use_global_device_ids=true, to_apply=%region_9.0 | all-reduce | flops 2 | bytes 16 | tf_op jit(solution)/shard_map/psum | solution.py:76
  551.1 10.2 %copy.31 = f32[32,128,512]{1,0,2:T(8,128)} copy(f32[32,128,512]{2,1,0:T(8,128)} %all-gather.7.cloned.1.call-done) | data formatting | bytes 16777216 | tf_op jit(solution)/shard_map/all_gather | solution.py:75
  561.3 9.0 %convolution_bitcast_fusion = f32[1,32]{1,0:T(1,128)S(1)} fusion(f32[128,512,1]{0,2,1:T(1,128)S(1)} %bitcast.132, f32[32,128,512]{1,0,2:T(8,128)} %copy.31), kind=kOutput, calls=%fused_computation.46 | convolution fusion | flops 25165824 | bytes 8650880 | tf_op jit(solution)/shard_map/krh,erh->ek/dot_general | solution.py:58
  570.3 9.2 %psum.29 = f32[1,32]{1,0:T(1,128)S(1)} all-reduce(f32[1,32]{1,0:T(1,128)S(1)} %convolution_bitcast_fusion), channel_id=1, replica_groups=mesh['layer'=2,'expert'=4,'col'=4] {'col'}, use_global_device_ids=true, to_apply=%region_5.0 | all-reduce | flops 32 | bytes 256 | tf_op jit(solution)/shard_map/psum | solution.py:58
  586.6 56.6 %all-gather.11.cloned.1.call-done = f32[32,128,512]{2,1,0:T(8,128)} async-done(((f32[8,128,512]{2,1,0:T(8,128)}), f32[32,128,512]{2,1,0:T(8,128)}) %all-gather.11.cloned.1.call-update) | async-done | bytes 8388624 | tf_op jit(solution)/shard_map/all_gather | solution.py:75
  643.3 8.4 %copy.37 = f32[32,128,512]{2,1,0:T(8,128)} copy(f32[32,128,512]{2,1,0:T(8,128)} %all-gather.11.cloned.1.call-done) | data formatting | bytes 16777216
  (48 shorter events, 40.7 us)
Async XLA Ops:
  7.2 77.2 %all-gather.5.cloned.1.call-start = ((), (), s32[]{:S(2)}) async-start(), calls=%async_computation.4 | async-start | bytes 4587520 | tf_op jit(solution)/shard_map/all_gather | solution.py:42
  7.9 187.5 %reduce-scatter.7.cloned.1.call-start = ((), (), s32[]{:S(2)}) async-start(), calls=%async_computation.6 | async-start | bytes 10485760 | tf_op jit(solution)/shard_map/reduce_scatter | solution.py:52
  84.4 24.5 %copy-start.4 = (f32[1,7168,128]{2,1,0:T(8,128)S(1)}, f32[1,7168,128]{2,1,0:T(8,128)}, u32[]{:S(2)}) copy-start(f32[1,7168,128]{2,1,0:T(8,128)} %all-gather.5.cloned.1.call-done) | copy-start | bytes 11010052
  103.7 5.2 copy-start.1
  108.9 11.9 %copy-start.7 = (f32[1,32]{1,0:T(1,128)S(1)}, f32[1,32]{1,0:T(1,128)}, u32[]{:S(2)}) copy-start(f32[1,32]{1,0:T(1,128)} %param.7) | copy-start | bytes 388
  125.3 141.0 %reduce-scatter.5.cloned.1.call-start = ((), (), s32[]{:S(2)}) async-start(), calls=%async_computation.5 | async-start | bytes 4587520 | tf_op jit(solution)/shard_map/reduce_scatter | solution.py:59
  139.2 60.9 %copy-start.5 = (f32[1,1792,128]{2,1,0:T(8,128)S(1)}, f32[1,1792,128]{2,1,0:T(8,128)}, u32[]{:S(2)}) copy-start(f32[1,1792,128]{2,1,0:T(8,128)} %param.5) | copy-start | bytes 2752516
  139.2 187.0 %all-gather.7.cloned.1.call-start = ((), (), s32[]{:S(2)}) async-start(), calls=%async_computation.7 | async-start | bytes 10485760 | tf_op jit(solution)/shard_map/all_gather | solution.py:75
  200.0 200.4 %all-gather.9.cloned.1.call-start = ((), (), s32[]{:S(2)}) async-start(), calls=%async_computation.8 | async-start | bytes 4587520 | tf_op jit(solution)/shard_map/all_gather | solution.py:42
  268.9 242.1 %reduce-scatter.11.cloned.1.call-start = ((), (), s32[]{:S(2)}) async-start(), calls=%async_computation.10 | async-start | bytes 10485760 | tf_op jit(solution)/shard_map/reduce_scatter | solution.py:52
  400.4 24.1 %copy-start.2 = (f32[1,7168,128]{1,2,0:T(8,128)S(1)}, f32[1,7168,128]{1,2,0:T(8,128)}, u32[]{:S(2)}) copy-start(f32[1,7168,128]{1,2,0:T(8,128)} %all-gather.9.cloned.1.call-done) | copy-start | bytes 11010052
  419.3 5.2 copy-start
  440.9 70.1 %copy-start.3 = (f32[8,128,512]{2,1,0:T(8,128)S(1)}, f32[8,128,512]{2,1,0:T(8,128)}, u32[]{:S(2)}) copy-start(f32[8,128,512]{2,1,0:T(8,128)} %divide_subtract_fusion) | copy-start | bytes 6291460
  440.9 142.3 %reduce-scatter.9.cloned.1.call-start = ((), (), s32[]{:S(2)}) async-start(), calls=%async_computation.9 | async-start | bytes 4587520 | tf_op jit(solution)/shard_map/reduce_scatter | solution.py:59
  455.0 188.3 %all-gather.11.cloned.1.call-start = ((), (), s32[]{:S(2)}) async-start(), calls=%async_computation.11 | async-start | bytes 10485760 | tf_op jit(solution)/shard_map/all_gather | solution.py:75
  561.3 21.8 %copy-start.6 = (f32[1792,1,128]{0,2,1:T(8,128)S(1)}, f32[1792,1,128]{0,2,1:T(8,128)}, u32[]{:S(2)}) copy-start(f32[1792,1,128]{0,2,1:T(8,128)} %reduce-scatter.5.cloned.1.call-done) | copy-start | bytes 2752516
Sparse Core Ops, SparseCore 0:
  9.5 74.8 all-gather.4
  125.4 69.9 reduce-scatter.6
  197.7 68.5 reduce-scatter.4
  267.7 58.5 all-gather.6
  328.3 72.0 all-gather.8
  441.0 69.9 reduce-scatter.10
  513.3 69.8 reduce-scatter.8
  584.7 58.5 all-gather.10
where the time goes:
time: 664 us; the launch traced here: 659 us
  waiting for transfers between devices  378 us (57%)
  matrix products  132 us (20%)
  blocking collectives  55.7 us (8%)
  local copies, waits for them, and re-layouts  51.6 us (8%)
  other arithmetic  25.9 us (4%)
  between operations  14.5 us (2%)
    all_gather x2, waiting for transfers between devices, shards(): gathered = lax.all_gather(current_factors, 'col', axis=1, tiled=True)  116 us
    reduce_scatter x2, waiting for transfers between devices, shards(): lax.psum_scatter(jnp.einsum('ek,erh->krh', coef_slice, d_pre, precision=H...  112 us
    all_gather x2, waiting for transfers between devices, shards(): current_bases = lax.all_gather(own_bases, 'expert', axis=0, tiled=True)  82.6 us
    reduce_scatter x2, waiting for transfers between devices, shards(): lax.psum_scatter(jnp.einsum('edh,erh->der', gradient, mixed, precision=HI...  67.1 us
    unnamed x21, local copies, waits for them, and re-layouts  40.9 us
    dot_general x2, matrix products, shards(): jnp.einsum('edr,erh->edh', gathered, mixed, precision=HIGHEST)  38.2 us
    psum x1, blocking collectives, shards(): loss_values.append(lax.psum(loss_part, ('expert', 'col')))  35 us
    dot_general x2, matrix products, shards(): jnp.einsum('edh,erh->der', gradient, mixed, precision=HIGHEST)  27.9 us
  transfers between devices with their start and end apart: 8, of which 8 were waited for; matrix products, arithmetic and copies ran while one was open for 18% of the time, Pallas kernels for 0%

commit v1 on v0

--- a/solution.py
+++ b/solution.py
@@ -39,7 +39,14 @@
     factor_two = jnp.zeros_like(factors)
     loss_values = []
     for iteration in range(ITERS):
-        gathered = lax.all_gather(current_factors, "col", axis=1, tiled=True)
+        ring = [current_factors]
+        for hop in range(3):
+            ring.append(lax.ppermute(ring[-1], "col", [(dev, (dev + 1) % 4) for dev in range(4)]))
+        gathered = jnp.roll(
+            jnp.concatenate(ring[::-1], axis=1),
+            (lax.axis_index("col") + 1) * ring[0].shape[1],
+            axis=1,
+        )
         mixed = jnp.tanh(jnp.einsum("ek,krh->erh", coefficients, current_bases, precision=HIGHEST))
         residual = jnp.einsum(
             "edr,erh->edh", gathered, mixed, precision=HIGHEST

time: 664 us -> 615 us (0.926)
  local copies, waits for them, and re-layouts: 51.6 us -> 10.8 us
  waiting for transfers between devices: 378 us -> 339 us
  other arithmetic: 25.9 us -> 54.4 us
  matrix products: 132 us -> 118 us
  blocking collectives: 55.7 us -> 64.8 us
    all_gather x2 -> x0, waiting for transfers between devices: 116 us -> none  [shards(): gathered = lax.all_gather(current_factors, 'col', axis=1, tiled=True)]
    ppermute x0 -> x6, waiting for transfers between devices: none -> 101 us  [shards(): lax.ppermute(ring[-1], 'col', [(dev, (dev + 1) % 4) for dev in range(4)])]
    unnamed x21, local copies, waits for them, and re-layouts: 40.9 us -> 10.8 us
    all_gather x2, waiting for transfers between devices: 82.6 us -> 57.1 us  [shards(): current_bases = lax.all_gather(own_bases, 'expert', axis=0, tiled=True)]
    another operation x0 -> x2, other arithmetic: none -> 20.9 us
    dot_general x2 -> x0, matrix products: 18.3 us -> none  [shards(): jnp.einsum('krh,erh->ek', current_bases, d_pre, precision=HIGHEST)]
    reduce_scatter x2, waiting for transfers between devices: 67.1 us -> 81.2 us  [shards(): lax.psum_scatter(jnp.einsum('edh,erh->der', gradient, mixed, precision=HI...]
    dot_general x2, matrix products: 27.9 us -> 40.1 us  [shards(): jnp.einsum('edh,erh->der', gradient, mixed, precision=HIGHEST)]
  transfers between devices with their start and end apart: 8 -> 12, of which waited for: 8 -> 10; matrix products, arithmetic and copies ran while one was open for 18% -> 14% of each run, Pallas kernels for 0% -> 0%
where the time goes in v1:
time: 615 us; the launch traced here: 607 us
  waiting for transfers between devices  339 us (55%)
  matrix products  118 us (19%)
  blocking collectives  64.8 us (11%)
  other arithmetic  54.4 us (9%)
  between operations  14.4 us (2%)
  local copies, waits for them, and re-layouts  10.8 us (2%)
    ppermute x6, waiting for transfers between devices, shards(): lax.ppermute(ring[-1], 'col', [(dev, (dev + 1) % 4) for dev in range(4)])  101 us
    reduce_scatter x2, waiting for transfers between devices, shards(): lax.psum_scatter(jnp.einsum('ek,erh->krh', coef_slice, d_pre, precision=H...  99.9 us
    reduce_scatter x2, waiting for transfers between devices, shards(): lax.psum_scatter(jnp.einsum('edh,erh->der', gradient, mixed, precision=HI...  81.2 us
    all_gather x2, waiting for transfers between devices, shards(): current_bases = lax.all_gather(own_bases, 'expert', axis=0, tiled=True)  57.1 us
    dot_general x2, matrix products, shards(): jnp.einsum('edh,erh->der', gradient, mixed, precision=HIGHEST)  40.1 us
    dot_general x2, matrix products, shards(): jnp.einsum('edr,erh->edh', gathered, mixed, precision=HIGHEST)  36 us
    psum x1, blocking collectives, shards(): loss_values.append(lax.psum(loss_part, ('expert', 'col')))  35 us
    psum x2, blocking collectives, shards(): lax.psum(jnp.einsum('krh,erh->ek', current_bases, d_pre, precision=HIGHES...  29.8 us
  transfers between devices with their start and end apart: 12, of which 10 were waited for; matrix products, arithmetic and copies ran while one was open for 14% of the time, Pallas kernels for 0%

profile of v1, /device:TPU:0, one launch (start us, length us, event | category | flops | bytes accessed | tf_op | source)
XLA Modules:
  0.0 607.0 jit_solution(2517056641889840278)
XLA Ops:
  10.3 22.6 %collective-permute-done = f32[1,1792,128]{2,1,0:T(8,128)S(1)} collective-permute-done((f32[1,1792,128]{2,1,0:T(8,128)}, f32[1,1792,128]{2,1,0:T(8,128)S(1)}, u32[]{:S(2)}, u32[]{:S(2)}) %collective-permute-start) | collective-permute-done | bytes 917536 | tf_op jit(solution)/shard_map/ppermute | solution.py:44
  32.9 23.3 %collective-permute-done.1 = f32[1,1792,128]{2,1,0:T(8,128)S(1)} collective-permute-done((f32[1,1792,128]{2,1,0:T(8,128)S(1)}, f32[1,1792,128]{2,1,0:T(8,128)S(1)}, u32[]{:S(2)}, u32[]{:S(2)}) %collective-permute-start.1) | collective-permute-done | bytes 917536 | tf_op jit(solution)/shard_map/ppermute | solution.py:44
  56.2 12.4 %fusion.20 = f32[1,128,512]{2,0,1:T(1,128)S(1)} fusion(f32[32,128,512]{2,1,0:T(8,128)} %param.8, f32[1,32]{1,0:T(1,128)} %param.9), kind=kOutput, calls=%fused_computation.22 | convolution fusion | flops 25165824 | bytes 8650880 | tf_op jit(solution)/shard_map/ek,krh->erh/dot_general | solution.py:50
  68.6 10.2 %collective-permute-done.2 = f32[1,1792,128]{2,1,0:T(8,128)} collective-permute-done((f32[1,1792,128]{2,1,0:T(8,128)S(1)}, f32[1,1792,128]{2,1,0:T(8,128)}, u32[]{:S(2)}, u32[]{:S(2)}) %collective-permute-start.2) | collective-permute-done | bytes 917536 | tf_op jit(solution)/shard_map/ppermute | solution.py:44
  78.8 12.0 %fusion.38 = f32[7168,128]{1,0:T(8,128)} fusion(s32[]{:T(128)S(6)} %select_n.17, f32[1,1792,128]{2,1,0:T(8,128)} %collective-permute-done.2, f32[1,1792,128]{2,1,0:T(8,128)S(1)} %collective-permute-done.1, f32[1,1792,128]{2,1,0:T(8,128)S(1)} %collective-permute-done, f32[1,1792,128]{2,1,0:T(8,128)S(1)} %copy-done.6), kind=kLoop, calls=%fused_computation.58 | loop fusion | flops 6422528 | bytes 7340036 | tf_op jit(solution)/shard_map/reshape.2
  90.8 18.3 %multiply_reduce_fusion.1 = (f32[]{:T(128)}, f32[1,7168,512]{2,1,0:T(8,128)S(1)}) fusion(bf16[1,7168,512]{2,1,0:T(8,128)(2,1)} %param.6, f32[7168,128]{1,0:T(8,128)} %fusion.38, f32[1,128,512]{2,0,1:T(1,128)S(1)} %fusion.20), kind=kOutput, calls=%fused_computation.11 | convolution fusion | flops 5651824640 | bytes 25952260 | tf_op jit(solution)/shard_map/edr,erh->edh/dot_general | solution.py:51
  109.1 9.2 %fusion.48 = f32[128,512]{1,0:T(8,128)S(1)} fusion(f32[7168,128]{1,0:T(8,128)S(1)} %copy-done.3, f32[1,7168,512]{2,1,0:T(8,128)S(1)} %get-tuple-element.18, f32[1,128,512]{2,0,1:T(1,128)S(1)} %fusion.20), kind=kOutput, calls=%fused_computation.73 | convolution fusion | flops 5641011200 | bytes 18874368 | tf_op jit(solution)/shard_map/edr,edh->erh/dot_general | solution.py:56
  122.9 20.1 %fusion.12 = f32[7168,1,128]{0,2,1:T(8,128)} fusion(f32[1,7168,512]{2,1,0:T(8,128)} %copy-done, f32[1,128,512]{2,0,1:T(1,128)S(1)} %fusion.20), kind=kOutput, calls=%fused_computation.16 | convolution fusion | flops 5640814592 | bytes 18612224 | tf_op jit(solution)/shard_map/edh,erh->der/dot_general | solution.py:67
  143.1 49.2 %reduce-scatter.7.cloned.1.call-done = f32[8,128,512]{2,1,0:T(8,128)} async-done(((f32[32,128,512]{2,1,0:T(8,128)}), f32[8,128,512]{2,1,0:T(8,128)}) %reduce-scatter.7.cloned.1.call-update) | async-done | bytes 2097168 | tf_op jit(solution)/shard_map/reduce_scatter | solution.py:59
  197.3 65.8 %reduce-scatter.5.cloned.1.call-done = f32[1792,1,128]{0,2,1:T(8,128)} async-done(((f32[7168,1,128]{0,2,1:T(8,128)}), f32[1792,1,128]{0,2,1:T(8,128)}) %reduce-scatter.5.cloned.1.call-update) | async-done | bytes 917520 | tf_op jit(solution)/shard_map/reduce_scatter | solution.py:66
  266.0 22.3 %collective-permute-done.3 = f32[1,1792,128]{1,2,0:T(8,128)S(1)} collective-permute-done((f32[1,1792,128]{1,2,0:T(8,128)S(1)}, f32[1,1792,128]{1,2,0:T(8,128)S(1)}, u32[]{:S(2)}, u32[]{:S(2)}) %collective-permute-start.3) | collective-permute-done | bytes 917536 | tf_op jit(solution)/shard_map/ppermute | solution.py:44
  289.2 22.8 %collective-permute-done.4 = f32[1,1792,128]{1,2,0:T(8,128)} collective-permute-done((f32[1,1792,128]{1,2,0:T(8,128)S(1)}, f32[1,1792,128]{1,2,0:T(8,128)}, u32[]{:S(2)}, u32[]{:S(2)}) %collective-permute-start.4) | collective-permute-done | bytes 917536 | tf_op jit(solution)/shard_map/ppermute | solution.py:44
  316.2 19.9 %psum.28 = f32[1,32]{1,0:T(1,128)S(1)} all-reduce(f32[1,32]{1,0:T(1,128)S(1)} %bitcast.106), channel_id=1, replica_groups=mesh['layer'=2,'expert'=4,'col'=4] {'col'}, use_global_device_ids=true, to_apply=%region_1.3 | all-reduce | flops 32 | bytes 256 | tf_op jit(solution)/shard_map/psum | solution.py:65
  336.1 8.9 %fusion.30 = f32[7168,128]{0,1:T(8,128)} fusion(s32[]{:T(128)S(6)} %select_n.17, f32[1,1792,128]{1,2,0:T(8,128)} %collective-permute-done.5, f32[1,1792,128]{1,2,0:T(8,128)} %collective-permute-done.4, f32[1,1792,128]{1,2,0:T(8,128)} %copy-done.7, f32[1,1792,128]{1,2,0:T(8,128)S(1)} %fusion.63), kind=kLoop, calls=%fused_computation.50 | loop fusion | flops 6422528 | bytes 7340036 | tf_op jit(solution)/shard_map/reshape.21
  345.0 12.4 %fusion.18 = f32[1,128,512]{2,0,1:T(1,128)S(1)} fusion(f32[32,128,512]{2,1,0:T(8,128)} %all-gather.3.cloned.1.call-done, f32[1,32]{1,0:T(1,128)S(1)} %divide_subtract_fusion.2), kind=kOutput, calls=%fused_computation.19 | convolution fusion | flops 25165824 | bytes 8650880 | tf_op jit(solution)/shard_map/ek,krh->erh/dot_general | solution.py:50
  357.4 17.7 %multiply_reduce_fusion = (f32[]{:T(128)}, f32[1,7168,512]{2,1,0:T(8,128)S(1)}) fusion(bf16[1,7168,512]{2,1,0:T(8,128)(2,1)} %param.6, f32[7168,128]{0,1:T(8,128)S(1)} %copy-done.2, f32[1,128,512]{2,0,1:T(1,128)S(1)} %fusion.18), kind=kOutput, calls=%fused_computation.10 | convolution fusion | flops 5651824640 | bytes 25952260 | tf_op jit(solution)/shard_map/edr,erh->edh/dot_general | solution.py:51
  375.1 8.4 %fusion.51 = f32[128,512]{1,0:T(8,128)S(1)} fusion(f32[7168,128]{0,1:T(8,128)S(1)} %copy-done.2, f32[1,7168,512]{2,1,0:T(8,128)S(1)} %get-tuple-element.16, f32[1,128,512]{2,0,1:T(1,128)S(1)} %fusion.18), kind=kOutput, calls=%fused_computation.74 | convolution fusion | flops 5641011200 | bytes 18874368 | tf_op jit(solution)/shard_map/edr,edh->erh/dot_general | solution.py:56
  388.1 20.1 %fusion.15 = f32[7168,1,128]{0,2,1:T(8,128)} fusion(f32[1,7168,512]{2,1,0:T(8,128)} %copy-done.1, f32[1,128,512]{2,0,1:T(1,128)S(1)} %fusion.18), kind=kOutput, calls=%fused_computation.17 | convolution fusion | flops 5640814592 | bytes 18612224 | tf_op jit(solution)/shard_map/edh,erh->der/dot_general | solution.py:67
  408.2 50.7 %reduce-scatter.11.cloned.1.call-done = f32[8,128,512]{2,1,0:T(8,128)} async-done(((f32[32,128,512]{2,1,0:T(8,128)}), f32[8,128,512]{2,1,0:T(8,128)}) %reduce-scatter.11.cloned.1.call-update) | async-done | bytes 2097168 | tf_op jit(solution)/shard_map/reduce_scatter | solution.py:59
  464.0 35.0 %all-reduce = (f32[1]{0:T(128)}, f32[1]{0:T(128)}) all-reduce(f32[1]{0:T(128)} %bitcast.26, f32[1]{0:T(128)} %bitcast.25), channel_id=1, replica_groups=mesh['layer'=2,'expert'=4,'col'=4] {'expert','col'}, use_global_device_ids=true, to_apply=%region_9.11 | all-reduce | flops 2 | bytes 16 | tf_op jit(solution)/shard_map/psum | solution.py:83
  503.3 9.9 %psum.29 = f32[1,32]{1,0:T(1,128)S(1)} all-reduce(f32[1,32]{1,0:T(1,128)S(1)} %bitcast.105), channel_id=1, replica_groups=mesh['layer'=2,'expert'=4,'col'=4] {'col'}, use_global_device_ids=true, to_apply=%region_5.7 | all-reduce | flops 32 | bytes 256 | tf_op jit(solution)/shard_map/psum | solution.py:65
  515.6 15.4 %reduce-scatter.9.cloned.1.call-done = f32[1792,1,128]{0,2,1:T(8,128)} async-done(((f32[7168,1,128]{0,2,1:T(8,128)}), f32[1792,1,128]{0,2,1:T(8,128)}) %reduce-scatter.9.cloned.1.call-update) | async-done | bytes 917520 | tf_op jit(solution)/shard_map/reduce_scatter | solution.py:66
  534.5 57.1 %all-gather.5.cloned.1.call-done = f32[32,128,512]{2,1,0:T(8,128)} async-done(((f32[8,128,512]{2,1,0:T(8,128)}), f32[32,128,512]{2,1,0:T(8,128)}) %all-gather.5.cloned.1.call-update) | async-done | bytes 8388624 | tf_op jit(solution)/shard_map/all_gather | solution.py:82
  591.5 8.4 %copy.47 = f32[32,128,512]{2,1,0:T(8,128)} copy(f32[32,128,512]{2,1,0:T(8,128)} %all-gather.5.cloned.1.call-done) | data formatting | bytes 16777216
  (51 shorter events, 40.7 us)
Async XLA Ops:
  7.2 185.1 %reduce-scatter.7.cloned.1.call-start = ((), (), s32[]{:S(2)}) async-start(), calls=%async_computation.5 | async-start | bytes 10485760 | tf_op jit(solution)/shard_map/reduce_scatter | solution.py:59
  7.2 25.7 %collective-permute-start = (f32[1,1792,128]{2,1,0:T(8,128)}, f32[1,1792,128]{2,1,0:T(8,128)S(1)}, u32[]{:S(2)}, u32[]{:S(2)}) collective-permute-start(f32[1,1792,128]{2,1,0:T(8,128)} %param.7), channel_id=1, source_target_pairs={{0,1},{1,2},{2,3},{3,0},{4,5},{5,6},{6,7},{7,4},{8,9},{9,10},{10,1... | collective-permute-start | bytes 2752520 | tf_op jit(solution)/shard_map/ppermute | solution.py:44
  32.9 23.3 %collective-permute-start.1 = (f32[1,1792,128]{2,1,0:T(8,128)S(1)}, f32[1,1792,128]{2,1,0:T(8,128)S(1)}, u32[]{:S(2)}, u32[]{:S(2)}) collective-permute-start(f32[1,1792,128]{2,1,0:T(8,128)S(1)} %collective-permute-done), channel_id=1, source_target_pairs={{0,1},{1,2},{2,3},{3,0},{4,5},{5,6},{6,7},{7,4},{8,9},{9,10},{10,1... | collective-permute-start | bytes 2752520 | tf_op jit(solution)/shard_map/ppermute | solution.py:44
  56.2 22.6 %collective-permute-start.2 = (f32[1,1792,128]{2,1,0:T(8,128)S(1)}, f32[1,1792,128]{2,1,0:T(8,128)}, u32[]{:S(2)}, u32[]{:S(2)}) collective-permute-start(f32[1,1792,128]{2,1,0:T(8,128)S(1)} %collective-permute-done.1), channel_id=1, source_target_pairs={{0,1},{1,2},{2,3},{3,0},{4,5},{5,6},{6,7},{7,4},{8,9},{9,10},{10,1... | collective-permute-start | bytes 2752520 | tf_op jit(solution)/shard_map/ppermute | solution.py:44
  56.2 22.6 %copy-start.6 = (f32[1,1792,128]{2,1,0:T(8,128)S(1)}, f32[1,1792,128]{2,1,0:T(8,128)}, u32[]{:S(2)}) copy-start(f32[1,1792,128]{2,1,0:T(8,128)} %param.7) | copy-start | bytes 2752516
  90.8 18.3 %copy-start.3 = (f32[7168,128]{1,0:T(8,128)S(1)}, f32[7168,128]{1,0:T(8,128)}, u32[]{:S(2)}) copy-start(f32[7168,128]{1,0:T(8,128)} %fusion.38) | copy-start | bytes 11010052
  109.1 9.2 %copy-start = (f32[1,7168,512]{2,1,0:T(8,128)}, f32[1,7168,512]{2,1,0:T(8,128)S(1)}, u32[]{:S(2)}) copy-start(f32[1,7168,512]{2,1,0:T(8,128)S(1)} %get-tuple-element.18) | copy-start | bytes 44040196
  109.1 9.2 %copy-start.8 = (f32[1,32]{1,0:T(1,128)S(1)}, f32[1,32]{1,0:T(1,128)}, u32[]{:S(2)}) copy-start(f32[1,32]{1,0:T(1,128)} %param.9) | copy-start | bytes 388
  122.9 140.2 %reduce-scatter.5.cloned.1.call-start = ((), (), s32[]{:S(2)}) async-start(), calls=%async_computation.4 | async-start | bytes 4587520 | tf_op jit(solution)/shard_map/reduce_scatter | solution.py:66
  143.0 201.9 %all-gather.3.cloned.1.call-start = ((), (), s32[]{:S(2)}) async-start(), calls=%async_computation.6 | async-start | bytes 10485760 | tf_op jit(solution)/shard_map/all_gather | solution.py:82
  196.9 262.1 %reduce-scatter.11.cloned.1.call-start = ((), (), s32[]{:S(2)}) async-start(), calls=%async_computation.8 | async-start | bytes 10485760 | tf_op jit(solution)/shard_map/reduce_scatter | solution.py:59
  264.7 23.6 %collective-permute-start.3 = (f32[1,1792,128]{1,2,0:T(8,128)S(1)}, f32[1,1792,128]{1,2,0:T(8,128)S(1)}, u32[]{:S(2)}, u32[]{:S(2)}) collective-permute-start(f32[1,1792,128]{1,2,0:T(8,128)S(1)} %fusion.63), channel_id=1, source_target_pairs={{0,1},{1,2},{2,3},{3,0},{4,5},{5,6},{6,7},{7,4},{8,9},{9,10},{10,1... | collective-permute-start | bytes 2752520 | tf_op jit(solution)/shard_map/ppermute | solution.py:44
  288.3 0.9 copy-start.7
  289.2 22.8 %collective-permute-start.4 = (f32[1,1792,128]{1,2,0:T(8,128)S(1)}, f32[1,1792,128]{1,2,0:T(8,128)}, u32[]{:S(2)}, u32[]{:S(2)}) collective-permute-start(f32[1,1792,128]{1,2,0:T(8,128)S(1)} %collective-permute-done.3), channel_id=1, source_target_pairs={{0,1},{1,2},{2,3},{3,0},{4,5},{5,6},{6,7},{7,4},{8,9},{9,10},{10,1... | collective-permute-start | bytes 2752520 | tf_op jit(solution)/shard_map/ppermute | solution.py:44
  312.0 24.1 %collective-permute-start.5 = (f32[1,1792,128]{1,2,0:T(8,128)}, f32[1,1792,128]{1,2,0:T(8,128)}, u32[]{:S(2)}, u32[]{:S(2)}) collective-permute-start(f32[1,1792,128]{1,2,0:T(8,128)} %collective-permute-done.4), channel_id=1, source_target_pairs={{0,1},{1,2},{2,3},{3,0},{4,5},{5,6},{6,7},{7,4},{8,9},{9,10},{10,1... | collective-permute-start | bytes 2752520 | tf_op jit(solution)/shard_map/ppermute | solution.py:44
  344.9 12.4 %copy-start.2 = (f32[7168,128]{0,1:T(8,128)S(1)}, f32[7168,128]{0,1:T(8,128)}, u32[]{:S(2)}) copy-start(f32[7168,128]{0,1:T(8,128)} %fusion.30) | copy-start | bytes 11010052
  375.1 8.4 %copy-start.1 = (f32[1,7168,512]{2,1,0:T(8,128)}, f32[1,7168,512]{2,1,0:T(8,128)S(1)}, u32[]{:S(2)}) copy-start(f32[1,7168,512]{2,1,0:T(8,128)S(1)} %get-tuple-element.16) | copy-start | bytes 44040196
  388.1 142.9 %reduce-scatter.9.cloned.1.call-start = ((), (), s32[]{:S(2)}) async-start(), calls=%async_computation.7 | async-start | bytes 4587520 | tf_op jit(solution)/shard_map/reduce_scatter | solution.py:66
  408.2 50.8 %copy-start.4 = (f32[8,128,512]{2,1,0:T(8,128)S(1)}, f32[8,128,512]{2,1,0:T(8,128)}, u32[]{:S(2)}) copy-start(f32[8,128,512]{2,1,0:T(8,128)} %divide_subtract_fusion) | copy-start | bytes 6291460
  408.2 183.3 %all-gather.5.cloned.1.call-start = ((), (), s32[]{:S(2)}) async-start(), calls=%async_computation.9 | async-start | bytes 10485760 | tf_op jit(solution)/shard_map/all_gather | solution.py:82
  499.0 32.0 %copy-start.5 = (f32[1792,1,128]{0,2,1:T(8,128)S(1)}, f32[1792,1,128]{0,2,1:T(8,128)}, u32[]{:S(2)}) copy-start(f32[1792,1,128]{0,2,1:T(8,128)} %reduce-scatter.5.cloned.1.call-done) | copy-start | bytes 2752516
Sparse Core Ops, SparseCore 0:
  123.0 69.1 reduce-scatter.6
  194.5 68.5 reduce-scatter.4
  264.7 58.5 all-gather.2
  388.2 70.7 reduce-scatter.10
  461.1 69.8 reduce-scatter.8
  533.0 58.4 all-gather.4
